TPU v7x, 128 devices: a whole 4x4x4 slice. The times are simulated.
128 devices in a mesh: sa: 4 (over x), sb: 2 (over core), sc: 16 (over z, y).
Axes of the slice: x: 4, y: 4, z: 4, core: 2. Of those that a mesh axis runs over, the one named last changes fastest.
Arguments:
- queries: float32 [65536, 2048], P(('sa', 'sb', 'sc')), may hold values from -6 to 6
- key_rows: float32 [65536, 2048], P(('sa', 'sb', 'sc')), may hold values from -6 to 6
- value_rows: float32 [65536, 2048], P(('sa', 'sb', 'sc')), may hold values from -6 to 6
- out_grad: float32 [65536, 2048], P(('sa', 'sb', 'sc')), may hold values from -6 to 6
- prefix_state: float32 [16, 128, 128], replicated, may hold values from -1536 to 1536
- suffix_state: float32 [16, 128, 128], replicated, may hold values from -1536 to 1536
Outputs:
- query_grad: bfloat16 [65536, 2048], P(('sa', 'sb', 'sc'))
- key_grad: bfloat16 [65536, 2048], P(('sa', 'sb', 'sc'))
- value_grad: bfloat16 [65536, 2048], P(('sa', 'sb', 'sc'))
All inputs are finite; a program needn't handle non-finite values.
Results may differ from a plain program's by a relative error of at most 0.0019.
Values sent between devices are 32-bit elements; how exact they have to be, the bound alone decides.
A program may use at most 576 MiB of HBM per device.

v0:
```python
import math
import jax
import jax.numpy as jnp
from jax import lax
from jax.sharding import PartitionSpec as P


def entering(part, axis, combine, identity):
    place = lax.axis_index(axis)
    gathered = jax.tree.map(lambda a: lax.all_gather(a, axis), part)
    state = jax.tree.map(lambda a, e: jnp.zeros_like(a) + jnp.asarray(e, a.dtype), part, identity)

    def one(hop, state):
        return combine(
            state, jax.tree.map(lambda a: lax.dynamic_index_in_dim(a, hop, 0, False), gathered)
        )

    return lax.fori_loop(0, place, one, state)


def add_states(earlier, later):
    return jax.tree.map(lambda left, right: left + right, earlier, later)


def run_chain(local_terms):
    zero_state = jax.tree.map(jnp.zeros_like, local_terms)
    inner_part = entering(local_terms, "sc", add_states, zero_state)
    group_sum = lax.psum((local_terms[0], local_terms[1]), "sc")
    middle_part = entering(group_sum, "sb", add_states, zero_state)
    block_sum = lax.psum((group_sum[0], group_sum[1]), "sb")
    outer_part = entering(block_sum, "sa", add_states, zero_state)
    return add_states(add_states(outer_part, middle_part), inner_part)


def shards(queries, key_rows, value_rows, out_grad, prefix_state, suffix_state):
    row_count = queries.shape[0]
    head_count = prefix_state.shape[0]
    head_size = prefix_state.shape[1]
    device_count = lax.axis_size("sa") * lax.axis_size("sb") * lax.axis_size("sc")
    factor = 1.0 / math.sqrt(head_size * row_count * device_count)
    highest = lax.Precision.HIGHEST
    shaped = (row_count, head_count, head_size)
    query_t = queries.reshape(shaped)
    key_t = key_rows.reshape(shaped)
    value_t = value_rows.reshape(shaped)
    grad_t = out_grad.reshape(shaped)
    kv_local = jnp.einsum("thd,the->hde", key_t, value_t, precision=highest)
    grad_local = jnp.einsum("the,thd->hed", grad_t, query_t, precision=highest)
    prior_kv, prior_grad = run_chain((kv_local, grad_local))
    total_grad = lax.psum(grad_local, ("sa", "sb", "sc"))
    state_before = prefix_state + prior_kv
    state_after = suffix_state + (total_grad - prior_grad - grad_local)
    lower = (
        lax.broadcasted_iota(jnp.int32, (row_count, row_count), 0)
        >= lax.broadcasted_iota(jnp.int32, (row_count, row_count), 1)
    ).astype(jnp.float32)
    grad_scores = jnp.einsum("the,she->hts", grad_t, value_t, precision=highest) * lower
    attn_scores = jnp.einsum("thd,shd->hts", query_t, key_t, precision=highest) * lower
    query_grad = factor * (
        jnp.einsum("the,hde->thd", grad_t, state_before, precision=highest)
        + jnp.einsum("hts,shd->thd", grad_scores, key_t, precision=highest)
    )
    key_grad = factor * (
        jnp.einsum("she,hed->shd", value_t, state_after, precision=highest)
        + jnp.einsum("hts,thd->shd", grad_scores, query_t, precision=highest)
    )
    value_grad = factor * (
        jnp.einsum("shd,hed->she", key_t, state_after, precision=highest)
        + jnp.einsum("hts,the->she", attn_scores, grad_t, precision=highest)
    )
    flat = (row_count, head_count * head_size)
    return (
        query_grad.astype(jnp.bfloat16).reshape(flat),
        key_grad.astype(jnp.bfloat16).reshape(flat),
        value_grad.astype(jnp.bfloat16).reshape(flat),
    )


def solution(mesh):
    return jax.shard_map(
        shards,
        mesh=mesh,
        in_specs=(
            P(("sa", "sb", "sc"), None),
            P(("sa", "sb", "sc"), None),
            P(("sa", "sb", "sc"), None),
            P(("sa", "sb", "sc"), None),
            P(),
            P(),
        ),
        out_specs=(
            P(("sa", "sb", "sc"), None),
            P(("sa", "sb", "sc"), None),
            P(("sa", "sb", "sc"), None),
        ),
        check_vma=False,
    )
```

profile of v0, /device:TPU:1, one launch (start us, length us, event | category | flops | bytes accessed | tf_op | source)
XLA Modules:
  0.0 613.8 jit_solution(8954921210702635121)
XLA Ops:
  8.0 11.2 %fusion.21 = f32[16,128,128]{2,1,0:T(8,128)} fusion(f32[512,2048]{1,0:T(8,128)} %param.14, f32[512,2048]{1,0:T(8,128)} %param.13), kind=kOutput, calls=%fused_computation.27 | convolution fusion | flops 1610612736 | bytes 9437184 | tf_op jit(solution)/shard_map/thd,the->hde/dot_general | solution.py:47
  19.2 5.1 copy.46
  24.3 5.7 copy.27
  30.1 9.2 %fusion.16 = f32[16,128,128]{2,1,0:T(8,128)} fusion(f32[512,16,128]{0,2,1:T(8,128)} %copy.27, f32[512,2048]{1,0:T(8,128)} %param.12), kind=kOutput, calls=%fused_computation.22 | convolution fusion | flops 1610612736 | bytes 9437184 | tf_op jit(solution)/shard_map/the,thd->hed/dot_general | solution.py:48
  39.3 94.8 %all-gather.19.cloned.1.call-done = f32[256,128,128]{2,1,0:T(8,128)} async-done(((f32[16,128,128]{2,1,0:T(8,128)}), f32[256,128,128]{2,1,0:T(8,128)}) %all-gather.19.cloned.1.call-update) | async-done | bytes 16777232 | tf_op jit(solution)/shard_map/all_gather | solution.py:10
  134.8 93.1 %all-reduce.8.cloned.1.call-done = (f32[16,128,128]{2,1,0:T(8,128)}, f32[16,128,128]{2,1,0:T(8,128)}) async-done(((f32[16,128,128]{2,1,0:T(8,128)}, f32[16,128,128]{2,1,0:T(8,128)}), (f32[16,128,128]{2,1,0:T(8,128)}, f32[16,128,128]{2,1,0:T(8,128)})) %all-reduce.8.cloned.1.call-update) | async-done | bytes 2097168 | tf_op jit(solution)/shard_map/psum | solution.py:28
  228.5 15.4 %all-gather.15.cloned.1.call-done = f32[32,128,128]{2,1,0:T(8,128)} async-done(((f32[16,128,128]{2,1,0:T(8,128)}), f32[32,128,128]{2,1,0:T(8,128)}) %all-gather.15.cloned.1.call-update) | async-done | bytes 2097168 | tf_op jit(solution)/shard_map/all_gather | solution.py:10
  243.9 16.3 %all-gather.17.cloned.1.call-done = f32[32,128,128]{2,1,0:T(8,128)} async-done(((f32[16,128,128]{2,1,0:T(8,128)}), f32[32,128,128]{2,1,0:T(8,128)}) %all-gather.17.cloned.1.call-update) | async-done | bytes 2097168 | tf_op jit(solution)/shard_map/all_gather | solution.py:10
  261.4 30.2 %all-reduce.10.cloned.1.call-done = (f32[1,16,128,128]{3,2,1,0:T(8,128)}, f32[1,16,128,128]{3,2,1,0:T(8,128)}) async-done(((f32[1,16,128,128]{3,2,1,0:T(8,128)}, f32[1,16,128,128]{3,2,1,0:T(8,128)}), (f32[1,16,128,128]{3,2,1,0:T(8,128)}, f32[1,16,128,128]{3,2,1,0:T(8,128)})) %all-reduce.10.cloned.1.call-update) | async-done | bytes 2097168 | tf_op jit(solution)/shard_map/psum | solution.py:30
  293.1 19.5 %fusion.14 = f32[16,512,512]{2,1,0:T(8,128)} fusion(f32[512,2048]{1,0:T(8,128)} %param.12, f32[512,2048]{1,0:T(8,128)} %param.13), kind=kOutput, calls=%fused_computation.20 | convolution fusion | flops 6442450944 | bytes 25165824 | tf_op jit(solution)/shard_map/thd,shd->hts/dot_general | solution.py:58
  312.6 14.5 %fusion.11 = f32[16,512,512]{2,1,0:T(8,128)S(1)} fusion(f32[512,2048]{1,0:T(8,128)S(1)} %copy-done.4, f32[512,2048]{1,0:T(8,128)S(1)} %copy-done.5), kind=kOutput, calls=%fused_computation.17 | convolution fusion | flops 6442450944 | bytes 25165824 | tf_op jit(solution)/shard_map/the,she->hts/dot_general | solution.py:57
  327.1 14.5 %fusion.2 = f32[16,512,128]{1,2,0:T(8,128)} fusion(f32[16,512,512]{2,1,0:T(8,128)S(1)} %fusion.11, f32[512,512]{1,0:T(8,128)S(1)} %fusion.55, f32[512,2048]{1,0:T(8,128)} %param.12), kind=kOutput, calls=%fused_computation.8 | convolution fusion | flops 6446645248 | bytes 26214400 | tf_op jit(solution)/shard_map/hts,thd->shd/dot_general | solution.py:65
  341.6 21.3 %fusion.4 = f32[16,512,128]{1,2,0:T(8,128)} fusion(f32[16,512,512]{2,1,0:T(8,128)S(1)} %fusion.11, f32[512,512]{1,0:T(8,128)S(1)} %fusion.55, f32[512,2048]{1,0:T(8,128)} %param.13), kind=kOutput, calls=%fused_computation.10 | convolution fusion | flops 6446645248 | bytes 26214400 | tf_op jit(solution)/shard_map/hts,shd->thd/dot_general | solution.py:61
  362.9 44.5 %all-gather.21.cloned.1.call-done = f32[256,128,128]{2,1,0:T(8,128)} async-done(((f32[16,128,128]{2,1,0:T(8,128)}), f32[256,128,128]{2,1,0:T(8,128)}) %all-gather.21.cloned.1.call-update) | async-done | bytes 16777232 | tf_op jit(solution)/shard_map/all_gather | solution.py:10
  410.9 45.8 %all-gather.11.cloned.1.call-done = f32[4,16,128,128]{3,2,1,0:T(8,128)} async-done(((f32[1,16,128,128]{3,2,1,0:T(8,128)}), f32[4,16,128,128]{3,2,1,0:T(8,128)}) %all-gather.11.cloned.1.call-update) | async-done | bytes 4194320 | tf_op jit(solution)/shard_map/all_gather | solution.py:10
  456.7 50.5 %all-gather.13.cloned.1.call-done = f32[4,16,128,128]{3,2,1,0:T(8,128)} async-done(((f32[1,16,128,128]{3,2,1,0:T(8,128)}), f32[4,16,128,128]{3,2,1,0:T(8,128)}) %all-gather.13.cloned.1.call-update) | async-done | bytes 4194320 | tf_op jit(solution)/shard_map/all_gather | solution.py:10
  508.4 44.6 %all-reduce.6.cloned.1.call-done = f32[16,128,128]{2,1,0:T(8,128)} async-done(((f32[16,128,128]{2,1,0:T(8,128)}), f32[16,128,128]{2,1,0:T(8,128)}) %all-reduce.6.cloned.1.call-update) | async-done | bytes 1048592 | tf_op jit(solution)/shard_map/psum | solution.py:50
  557.5 3.8 fusion.23
  561.3 14.6 %fusion.29 = bf16[512,16,128]{0,2,1:T(8,128)(2,1)} fusion(f32[16,128,512]{2,1,0:T(8,128)S(1)} %fusion.23, f32[512,16,128]{0,2,1:T(8,128)S(1)} %copy-done.3, f32[16,512,512]{2,1,0:T(8,128)} %fusion.14, f32[512,512]{1,0:T(8,128)S(1)} %copy-done.7), kind=kOutput, calls=%fused_computation.36 | convolution fusion | flops 6449790976 | bytes 28311552 | tf_op jit(solution)/shard_map/hts,the->she/dot_general | solution.py:69
  575.9 3.9 copy.40
  579.8 9.2 %fusion.31 = bf16[512,16,128]{0,2,1:T(8,128)(2,1)} fusion(f32[16,512,128]{1,2,0:T(8,128)} %fusion.2, f32[16,128,128]{2,1,0:T(8,128)} %copy-done.8, f32[512,2048]{1,0:T(8,128)} %param.14), kind=kOutput, calls=%fused_computation.39 | convolution fusion | flops 1613758464 | bytes 11534336 | tf_op jit(solution)/shard_map/she,hed->shd/dot_general | solution.py:64
  589.0 4.1 copy.39
  593.1 9.2 %fusion.33 = bf16[512,16,128]{0,2,1:T(8,128)(2,1)} fusion(f32[16,512,128]{1,2,0:T(8,128)} %fusion.4, f32[16,128,128]{2,1,0:T(8,128)} %param.16, f32[16,128,128]{2,1,0:T(8,128)S(1)} %get-tuple-element.107, f32[16,128,128]{2,1,0:T(8,128)S(1)} %get-tuple-element.105, f32[16,128,128]{2,1,0:T(8,128)S(1)} %get-tuple-element.106, f32[512,2048]{1,0:T(8,128)} %param.15), kind=kOutput, calls=%fused_computation.42 | convolution fusion | flops 1614544896 | bytes 14680064 | tf_op jit(solution)/shard_map/the,hde->thd/dot_general | solution.py:60
  602.3 3.9 copy.38
  (48 shorter events, 15.3 us)
Async XLA Ops:
  8.0 126.0 %all-gather.19.cloned.1.call-start = ((), (), s32[]{:S(2)}) async-start(), calls=%async_computation.5 | async-start | bytes 17825792 | tf_op jit(solution)/shard_map/all_gather | solution.py:10
  134.0 93.9 %all-reduce.8.cloned.1.call-start = ((), (), s32[]{:S(2)}) async-start(), calls=%async_computation.7 | async-start | bytes 4194304 | tf_op jit(solution)/shard_map/psum | solution.py:28
  134.8 109.2 %all-gather.15.cloned.1.call-start = ((), (), s32[]{:S(2)}) async-start(), calls=%async_computation.3 | async-start | bytes 3145728 | tf_op jit(solution)/shard_map/all_gather | solution.py:10
  228.0 32.2 %all-gather.17.cloned.1.call-start = ((), (), s32[]{:S(2)}) async-start(), calls=%async_computation.4 | async-start | bytes 3145728 | tf_op jit(solution)/shard_map/all_gather | solution.py:10
  260.2 31.4 %all-reduce.10.cloned.1.call-start = ((), (), s32[]{:S(2)}) async-start(), calls=%async_computation.8 | async-start | bytes 4194304 | tf_op jit(solution)/shard_map/psum | solution.py:30
  260.8 146.6 %all-gather.21.cloned.1.call-start = ((), (), s32[]{:S(2)}) async-start(), calls=%async_computation.6 | async-start | bytes 17825792 | tf_op jit(solution)/shard_map/all_gather | solution.py:10
  261.4 195.3 %all-gather.11.cloned.1.call-start = ((), (), s32[]{:S(2)}) async-start(), calls=%async_computation | async-start | bytes 5242880 | tf_op jit(solution)/shard_map/all_gather | solution.py:10
  291.6 215.6 %all-gather.13.cloned.1.call-start = ((), (), s32[]{:S(2)}) async-start(), calls=%async_computation.1 | async-start | bytes 5242880 | tf_op jit(solution)/shard_map/all_gather | solution.py:10
  292.3 260.6 %all-reduce.6.cloned.1.call-start = ((), (), s32[]{:S(2)}) async-start(), calls=%async_computation.2 | async-start | bytes 2097152 | tf_op jit(solution)/shard_map/psum | solution.py:50
  293.0 48.6 %copy-start.6 = (f32[512,512]{1,0:T(8,128)}, f32[512,512]{1,0:T(8,128)S(1)}, u32[]{:S(2)}) copy-start(f32[512,512]{1,0:T(8,128)S(1)} %fusion.55) | copy-start | bytes 3145732
  293.1 19.6 %copy-start.4 = (f32[512,2048]{1,0:T(8,128)S(1)}, f32[512,2048]{1,0:T(8,128)}, u32[]{:S(2)}) copy-start(f32[512,2048]{1,0:T(8,128)} %param.15) | copy-start | bytes 12582916
  293.1 19.6 %copy-start.5 = (f32[512,2048]{1,0:T(8,128)S(1)}, f32[512,2048]{1,0:T(8,128)}, u32[]{:S(2)}) copy-start(f32[512,2048]{1,0:T(8,128)} %param.14) | copy-start | bytes 12582916
  407.6 1.0 copy-start.1
  410.9 45.8 %copy-start.2 = (f32[16,128,128]{2,1,0:T(8,128)}, f32[16,128,128]{2,1,0:T(8,128)S(1)}, u32[]{:S(2)}) copy-start(f32[16,128,128]{2,1,0:T(8,128)S(1)} %get-tuple-element.109) | copy-start | bytes 3145732
  552.9 4.5 copy-start
  556.4 1.0 copy-start.8
  557.5 3.8 copy-start.3
  557.5 3.8 copy-start.7
Sparse Core Ops, SparseCore 0:
  19.4 114.6 all-gather.18
  138.8 89.0 all-reduce.7
  229.7 14.2 all-gather.14
  245.5 14.6 all-gather.16
  263.4 28.1 all-reduce.9
  294.1 113.1 all-gather.20
  409.0 47.6 all-gather.10
  458.3 48.7 all-gather.12
Sparse Core Ops, SparseCore 1:
  298.2 254.7 all-reduce.5
where the time goes:
time: 621 us; the launch traced here: 614 us
  waiting for transfers between devices  439 us (71%)
  matrix products  127 us (20%)
  local copies, waits for them, and re-layouts  26.3 us (4%)
  between operations  16 us (3%)
    all_gather x6, waiting for transfers between devices, entering(): gathered = jax.tree.map(lambda a: lax.all_gather(a, axis), part)  267 us
    psum x1, waiting for transfers between devices, run_chain(): group_sum = lax.psum((local_terms[0], local_terms[1]), 'sc')  93.1 us
    psum x1, waiting for transfers between devices, shards(): total_grad = lax.psum(grad_local, ('sa', 'sb', 'sc'))  44.6 us
    psum x1, waiting for transfers between devices, run_chain(): block_sum = lax.psum((group_sum[0], group_sum[1]), 'sb')  30.2 us
    dot_general x1, matrix products, shards(): jnp.einsum('hts,shd->thd', grad_scores, key_t, precision=highest)  21.3 us
    dot_general x1, matrix products, shards(): jnp.einsum('thd,shd->hts', query_t, key_t, precision=highest) * lower  19.5 us
    unnamed x22, local copies, waits for them, and re-layouts  19 us
    dot_general x1, matrix products, shards(): jnp.einsum('hts,the->she', attn_scores, grad_t, precision=highest)  14.6 us
  transfers between devices with their start and end apart: 9, of which 9 were waited for; matrix products, arithmetic and copies ran while one was open for 15% of the time, Pallas kernels for 0%

commit v1 on v0

--- a/solution.py
+++ b/solution.py
@@ -47,7 +47,9 @@
     kv_local = jnp.einsum("thd,the->hde", key_t, value_t, precision=highest)
     grad_local = jnp.einsum("the,thd->hed", grad_t, query_t, precision=highest)
     prior_kv, prior_grad = run_chain((kv_local, grad_local))
-    total_grad = lax.psum(grad_local, ("sa", "sb", "sc"))
+    total_grad = grad_local
+    for mesh_axis in (("sb", "sc"), "sa"):
+        total_grad = lax.psum(total_grad, mesh_axis)
     state_before = prefix_state + prior_kv
     state_after = suffix_state + (total_grad - prior_grad - grad_local)
     lower = (

time: 621 us -> 729 us (1.17)
  waiting for transfers between devices: 439 us -> 548 us
    all_gather x6, waiting for transfers between devices: 267 us -> 337 us  [entering(): gathered = jax.tree.map(lambda a: lax.all_gather(a, axis), part)]
    psum x1 -> x2, waiting for transfers between devices: 44.6 us -> 84.7 us  [shards(): total_grad = lax.psum(total_grad, mesh_axis)]
  transfers between devices with their start and end apart: 9 -> 10, of which waited for: 9 -> 10; matrix products, arithmetic and copies ran while one was open for 15% -> 13% of each run, Pallas kernels for 0% -> 0%
where the time goes in v1:
time: 729 us; the launch traced here: 722 us
  waiting for transfers between devices  548 us (75%)
  matrix products  127 us (17%)
  local copies, waits for them, and re-layouts  26.3 us (4%)
  between operations  14.6 us (2%)
    all_gather x6, waiting for transfers between devices, entering(): gathered = jax.tree.map(lambda a: lax.all_gather(a, axis), part)  337 us
    psum x1, waiting for transfers between devices, run_chain(): group_sum = lax.psum((local_terms[0], local_terms[1]), 'sc')  93.1 us
    psum x2, waiting for transfers between devices, shards(): total_grad = lax.psum(total_grad, mesh_axis)  84.7 us
    psum x1, waiting for transfers between devices, run_chain(): block_sum = lax.psum((group_sum[0], group_sum[1]), 'sb')  29.4 us
    dot_general x1, matrix products, shards(): jnp.einsum('hts,shd->thd', grad_scores, key_t, precision=highest)  20.9 us
    dot_general x1, matrix products, shards(): jnp.einsum('thd,shd->hts', query_t, key_t, precision=highest) * lower  19.5 us
    unnamed x22, local copies, waits for them, and re-layouts  19 us
    dot_general x1, matrix products, shards(): jnp.einsum('hts,thd->shd', grad_scores, query_t, precision=highest)  14.8 us
  transfers between devices with their start and end apart: 10, of which 10 were waited for; matrix products, arithmetic and copies ran while one was open for 13% of the time, Pallas kernels for 0%

profile of v1, /device:TPU:1, one launch (start us, length us, event | category | flops | bytes accessed | tf_op | source)
XLA Modules:
  0.0 721.8 jit_solution(10570711667916914884)
XLA Ops:
  7.2 11.2 %fusion.21 = f32[16,128,128]{2,1,0:T(8,128)} fusion(f32[512,2048]{1,0:T(8,128)} %param.14, f32[512,2048]{1,0:T(8,128)} %param.13), kind=kOutput, calls=%fused_computation.27 | convolution fusion | flops 1610612736 | bytes 9437184 | tf_op jit(solution)/shard_map/thd,the->hde/dot_general | solution.py:47
  18.4 5.1 copy.46
  23.5 5.7 copy.27
  29.2 9.2 %fusion.16 = f32[16,128,128]{2,1,0:T(8,128)} fusion(f32[512,16,128]{0,2,1:T(8,128)} %copy.27, f32[512,2048]{1,0:T(8,128)} %param.12), kind=kOutput, calls=%fused_computation.22 | convolution fusion | flops 1610612736 | bytes 9437184 | tf_op jit(solution)/shard_map/the,thd->hed/dot_general | solution.py:48
  38.4 94.8 %all-gather.19.cloned.1.call-done = f32[256,128,128]{2,1,0:T(8,128)} async-done(((f32[16,128,128]{2,1,0:T(8,128)}), f32[256,128,128]{2,1,0:T(8,128)}) %all-gather.19.cloned.1.call-update) | async-done | bytes 16777232 | tf_op jit(solution)/shard_map/all_gather | solution.py:10
  134.0 93.1 %all-reduce.11.cloned.1.call-done = (f32[16,128,128]{2,1,0:T(8,128)}, f32[16,128,128]{2,1,0:T(8,128)}) async-done(((f32[16,128,128]{2,1,0:T(8,128)}, f32[16,128,128]{2,1,0:T(8,128)}), (f32[16,128,128]{2,1,0:T(8,128)}, f32[16,128,128]{2,1,0:T(8,128)})) %all-reduce.11.cloned.1.call-update) | async-done | bytes 2097168 | tf_op jit(solution)/shard_map/psum | solution.py:28
  227.7 15.4 %all-gather.15.cloned.1.call-done = f32[32,128,128]{2,1,0:T(8,128)} async-done(((f32[16,128,128]{2,1,0:T(8,128)}), f32[32,128,128]{2,1,0:T(8,128)}) %all-gather.15.cloned.1.call-update) | async-done | bytes 2097168 | tf_op jit(solution)/shard_map/all_gather | solution.py:10
  243.1 16.3 %all-gather.17.cloned.1.call-done = f32[32,128,128]{2,1,0:T(8,128)} async-done(((f32[16,128,128]{2,1,0:T(8,128)}), f32[32,128,128]{2,1,0:T(8,128)}) %all-gather.17.cloned.1.call-update) | async-done | bytes 2097168 | tf_op jit(solution)/shard_map/all_gather | solution.py:10
  261.3 29.4 %all-reduce.13.cloned.1.call-done = (f32[1,16,128,128]{3,2,1,0:T(8,128)}, f32[1,16,128,128]{3,2,1,0:T(8,128)}) async-done(((f32[1,16,128,128]{3,2,1,0:T(8,128)}, f32[1,16,128,128]{3,2,1,0:T(8,128)}), (f32[1,16,128,128]{3,2,1,0:T(8,128)}, f32[1,16,128,128]{3,2,1,0:T(8,128)})) %all-reduce.13.cloned.1.call-update) | async-done | bytes 2097168 | tf_op jit(solution)/shard_map/psum | solution.py:30
  291.7 19.5 %fusion.14 = f32[16,512,512]{2,1,0:T(8,128)} fusion(f32[512,2048]{1,0:T(8,128)} %param.12, f32[512,2048]{1,0:T(8,128)} %param.13), kind=kOutput, calls=%fused_computation.20 | convolution fusion | flops 6442450944 | bytes 25165824 | tf_op jit(solution)/shard_map/thd,shd->hts/dot_general | solution.py:60
  311.3 14.5 %fusion.11 = f32[16,512,512]{2,1,0:T(8,128)S(1)} fusion(f32[512,2048]{1,0:T(8,128)S(1)} %copy-done.4, f32[512,2048]{1,0:T(8,128)S(1)} %copy-done.5), kind=kOutput, calls=%fused_computation.17 | convolution fusion | flops 6442450944 | bytes 25165824 | tf_op jit(solution)/shard_map/the,she->hts/dot_general | solution.py:59
  325.7 20.9 %fusion.4 = f32[16,512,128]{1,2,0:T(8,128)} fusion(f32[16,512,512]{2,1,0:T(8,128)S(1)} %fusion.11, f32[512,512]{1,0:T(8,128)S(1)} %fusion.55, f32[512,2048]{1,0:T(8,128)} %param.13), kind=kOutput, calls=%fused_computation.10 | convolution fusion | flops 6446645248 | bytes 26214400 | tf_op jit(solution)/shard_map/hts,shd->thd/dot_general | solution.py:63
  346.7 14.8 %fusion.2 = f32[16,512,128]{1,2,0:T(8,128)} fusion(f32[16,512,512]{2,1,0:T(8,128)S(1)} %fusion.11, f32[512,512]{1,0:T(8,128)S(1)} %fusion.55, f32[512,2048]{1,0:T(8,128)} %param.12), kind=kOutput, calls=%fused_computation.8 | convolution fusion | flops 6446645248 | bytes 26214400 | tf_op jit(solution)/shard_map/hts,thd->shd/dot_general | solution.py:67
  361.5 38.8 %all-reduce.7.cloned.1.call-done = f32[16,128,128]{2,1,0:T(8,128)} async-done(((f32[16,128,128]{2,1,0:T(8,128)}), f32[16,128,128]{2,1,0:T(8,128)}) %all-reduce.7.cloned.1.call-update) | async-done | bytes 1048592 | tf_op jit(solution)/shard_map/psum | solution.py:52
  400.3 114.1 %all-gather.21.cloned.1.call-done = f32[256,128,128]{2,1,0:T(8,128)} async-done(((f32[16,128,128]{2,1,0:T(8,128)}), f32[256,128,128]{2,1,0:T(8,128)}) %all-gather.21.cloned.1.call-update) | async-done | bytes 16777232 | tf_op jit(solution)/shard_map/all_gather | solution.py:10
  518.0 46.1 %all-gather.11.cloned.1.call-done = f32[4,16,128,128]{3,2,1,0:T(8,128)} async-done(((f32[1,16,128,128]{3,2,1,0:T(8,128)}), f32[4,16,128,128]{3,2,1,0:T(8,128)}) %all-gather.11.cloned.1.call-update) | async-done | bytes 4194320 | tf_op jit(solution)/shard_map/all_gather | solution.py:10
  564.1 50.4 %all-gather.13.cloned.1.call-done = f32[4,16,128,128]{3,2,1,0:T(8,128)} async-done(((f32[1,16,128,128]{3,2,1,0:T(8,128)}), f32[4,16,128,128]{3,2,1,0:T(8,128)}) %all-gather.13.cloned.1.call-update) | async-done | bytes 4194320 | tf_op jit(solution)/shard_map/all_gather | solution.py:10
  615.7 45.9 %all-reduce.9.cloned.1.call-done = f32[16,128,128]{2,1,0:T(8,128)} async-done(((f32[16,128,128]{2,1,0:T(8,128)}), f32[16,128,128]{2,1,0:T(8,128)}) %all-reduce.9.cloned.1.call-update) | async-done | bytes 1048592 | tf_op jit(solution)/shard_map/psum | solution.py:52
  669.9 14.6 %fusion.29 = bf16[512,16,128]{0,2,1:T(8,128)(2,1)} fusion(f32[16,128,512]{2,1,0:T(8,128)S(1)} %fusion.23, f32[512,16,128]{0,2,1:T(8,128)S(1)} %copy-done.3, f32[16,512,512]{2,1,0:T(8,128)} %fusion.14, f32[512,512]{1,0:T(8,128)S(1)} %copy-done.7), kind=kOutput, calls=%fused_computation.36 | convolution fusion | flops 6449790976 | bytes 28311552 | tf_op jit(solution)/shard_map/hts,the->she/dot_general | solution.py:71
  684.5 3.9 copy.40
  688.4 9.2 %fusion.31 = bf16[512,16,128]{0,2,1:T(8,128)(2,1)} fusion(f32[16,512,128]{1,2,0:T(8,128)} %fusion.2, f32[16,128,128]{2,1,0:T(8,128)} %copy-done.8, f32[512,2048]{1,0:T(8,128)} %param.14), kind=kOutput, calls=%fused_computation.39 | convolution fusion | flops 1613758464 | bytes 11534336 | tf_op jit(solution)/shard_map/she,hed->shd/dot_general | solution.py:66
  697.6 4.1 copy.39
  701.7 9.2 %fusion.33 = bf16[512,16,128]{0,2,1:T(8,128)(2,1)} fusion(f32[16,512,128]{1,2,0:T(8,128)} %fusion.4, f32[16,128,128]{2,1,0:T(8,128)} %param.16, f32[16,128,128]{2,1,0:T(8,128)S(1)} %get-tuple-element.107, f32[16,128,128]{2,1,0:T(8,128)S(1)} %get-tuple-element.105, f32[16,128,128]{2,1,0:T(8,128)S(1)} %get-tuple-element.106, f32[512,2048]{1,0:T(8,128)} %param.15), kind=kOutput, calls=%fused_computation.42 | convolution fusion | flops 1614544896 | bytes 14680064 | tf_op jit(solution)/shard_map/the,hde->thd/dot_general | solution.py:62
  710.9 3.9 copy.38
  (51 shorter events, 19.3 us)
Async XLA Ops:
  7.2 126.0 %all-gather.19.cloned.1.call-start = ((), (), s32[]{:S(2)}) async-start(), calls=%async_computation.6 | async-start | bytes 17825792 | tf_op jit(solution)/shard_map/all_gather | solution.py:10
  133.2 93.9 %all-reduce.11.cloned.1.call-start = ((), (), s32[]{:S(2)}) async-start(), calls=%async_computation.8 | async-start | bytes 4194304 | tf_op jit(solution)/shard_map/psum | solution.py:28
  133.9 109.2 %all-gather.15.cloned.1.call-start = ((), (), s32[]{:S(2)}) async-start(), calls=%async_computation.4 | async-start | bytes 3145728 | tf_op jit(solution)/shard_map/all_gather | solution.py:10
  227.1 32.2 %all-gather.17.cloned.1.call-start = ((), (), s32[]{:S(2)}) async-start(), calls=%async_computation.5 | async-start | bytes 3145728 | tf_op jit(solution)/shard_map/all_gather | solution.py:10
  259.4 31.4 %all-reduce.13.cloned.1.call-start = ((), (), s32[]{:S(2)}) async-start(), calls=%async_computation.9 | async-start | bytes 4194304 | tf_op jit(solution)/shard_map/psum | solution.py:30
  259.9 140.4 %all-reduce.7.cloned.1.call-start = ((), (), s32[]{:S(2)}) async-start(), calls=%async_computation.2 | async-start | bytes 2097152 | tf_op jit(solution)/shard_map/psum | solution.py:52
  260.5 253.9 %all-gather.21.cloned.1.call-start = ((), (), s32[]{:S(2)}) async-start(), calls=%async_computation.7 | async-start | bytes 17825792 | tf_op jit(solution)/shard_map/all_gather | solution.py:10
  261.3 302.8 %all-gather.11.cloned.1.call-start = ((), (), s32[]{:S(2)}) async-start(), calls=%async_computation | async-start | bytes 5242880 | tf_op jit(solution)/shard_map/all_gather | solution.py:10
  290.8 323.7 %all-gather.13.cloned.1.call-start = ((), (), s32[]{:S(2)}) async-start(), calls=%async_computation.1 | async-start | bytes 5242880 | tf_op jit(solution)/shard_map/all_gather | solution.py:10
  291.5 370.1 %all-reduce.9.cloned.1.call-start = ((), (), s32[]{:S(2)}) async-start(), calls=%async_computation.3 | async-start | bytes 2097152 | tf_op jit(solution)/shard_map/psum | solution.py:52
  291.7 55.0 %copy-start.6 = (f32[512,512]{1,0:T(8,128)}, f32[512,512]{1,0:T(8,128)S(1)}, u32[]{:S(2)}) copy-start(f32[512,512]{1,0:T(8,128)S(1)} %fusion.55) | copy-start | bytes 3145732
  291.7 19.6 %copy-start.4 = (f32[512,2048]{1,0:T(8,128)S(1)}, f32[512,2048]{1,0:T(8,128)}, u32[]{:S(2)}) copy-start(f32[512,2048]{1,0:T(8,128)} %param.15) | copy-start | bytes 12582916
  291.7 19.6 %copy-start.5 = (f32[512,2048]{1,0:T(8,128)S(1)}, f32[512,2048]{1,0:T(8,128)}, u32[]{:S(2)}) copy-start(f32[512,2048]{1,0:T(8,128)} %param.14) | copy-start | bytes 12582916
  514.7 1.0 copy-start.1
  518.0 46.1 %copy-start.2 = (f32[16,128,128]{2,1,0:T(8,128)}, f32[16,128,128]{2,1,0:T(8,128)S(1)}, u32[]{:S(2)}) copy-start(f32[16,128,128]{2,1,0:T(8,128)S(1)} %get-tuple-element.109) | copy-start | bytes 3145732
  661.5 4.5 copy-start
  665.1 1.0 copy-start.8
  666.1 3.8 copy-start.3
  666.1 3.8 copy-start.7
Sparse Core Ops, SparseCore 0:
  18.5 114.6 all-gather.18
  138.0 89.0 all-reduce.10
  228.9 14.2 all-gather.14
  244.7 14.6 all-gather.16
  262.5 28.1 all-reduce.12
  294.4 105.8 all-reduce.6
  403.2 111.1 all-gather.20
  516.2 47.8 all-gather.10
  565.9 48.5 all-gather.12
  616.8 44.7 all-reduce.8
